TPU v7x, 256 devices: a whole 4x4x8 slice. The times are simulated.
256 devices in a mesh: ka: 16 (over y_lo, z), br: 4 (over y_hi, core), bc: 4 (over x).
Axes of the slice: x: 4, y: 4 (y_hi: 2, y_lo: 2; y = y_hi * 2 + y_lo), z: 8, core: 2. Of those that a mesh axis runs over, the one named last changes fastest.
Arguments:
- green_lesser: float32 [16, 15, 2, 512, 512], P('ka', None, None, 'br', 'bc'), may hold values from -6 to 6
- screened: float32 [5, 8, 2, 512, 512], P(None, None, None, 'br', 'bc'), may hold values from -0.6 to 0.6
- slot_table: int32 [5, 16, 1], P(None, 'ka'), may hold values from 0 to 4
Outputs:
- sigma_lesser: float32 [16, 8, 2, 512, 512], P('ka', None, None, 'br', 'bc')
All inputs are finite; a program needn't handle non-finite values.
Results may differ from a plain program's by a relative error of at most 0.0003.
Values sent between devices are 32-bit elements; how exact they have to be, the bound alone decides.
A program may use at most 64 MiB of HBM per device.

v0:
```python
import jax
import jax.numpy as jnp
from jax import lax
from jax.sharding import PartitionSpec as P

NE = 8


def sent_to_all(x, axis):
    copies = jnp.broadcast_to(x, (lax.axis_size(axis), *x.shape))
    return lax.all_to_all(copies, axis, split_axis=0, concat_axis=0, tiled=True)


def laid_out(blocks, dim):
    blocks = jnp.moveaxis(blocks, 0, dim)
    shape = blocks.shape
    return blocks.reshape(*shape[:dim], shape[dim] * shape[dim + 1], *shape[dim + 2 :])


def collect(x, axis, dim):
    blocks = sent_to_all(x, axis)
    return laid_out(blocks, dim)


def shifted(x, axis, by):
    size = lax.axis_size(axis)
    return lax.ppermute(x, axis, [(i, (i + by) % size) for i in range(size)])


def stop_terms(remote, slot_row, screened, energies):
    freq_count = screened.shape[1]
    real_sum = jnp.zeros((energies,) + remote.shape[3:], jnp.float32)
    imag_sum = jnp.zeros((energies,) + remote.shape[3:], jnp.float32)
    chosen = lax.dynamic_index_in_dim(screened, slot_row[0, 0], 0, keepdims=False)
    for freq_index in range(freq_count):
        lag_start = freq_count - 1 - freq_index
        window = remote[0, lag_start : lag_start + energies]
        green_real = window[:, 0]
        green_imag = window[:, 1]
        inter_real = chosen[freq_index, 0]
        inter_imag = chosen[freq_index, 1]
        real_sum = real_sum - (green_real * inter_imag + green_imag * inter_real)
        imag_sum = imag_sum + (green_real * inter_real - green_imag * inter_imag)
    blocks_out = [jnp.stack((real_sum, imag_sum), 1)]
    return jnp.stack(blocks_out, 0)


def on_device(green_lesser, screened, slot_table):
    own_count = green_lesser.shape[0]
    full_slots = collect(slot_table, "ka", 1)
    here = lax.axis_index("ka")
    loop_size = lax.axis_size("ka")

    def target_terms(offset, stop_index):
        start = (here + offset) % loop_size * own_count
        rows = lax.dynamic_slice_in_dim(full_slots[stop_index], start, own_count, 0)
        return stop_terms(green_lesser, rows, screened, NE)

    accumulated = stop_terms(green_lesser, slot_table[0], screened, NE)
    rising = target_terms(2, 3)
    falling = target_terms(-2, 4)
    for step_number in range(2):
        rising = shifted(rising, "ka", 1)
        falling = shifted(falling, "ka", -1)
        if step_number == 0:
            rising = rising + target_terms(1, 1)
            falling = falling + target_terms(-1, 2)
    accumulated = accumulated + rising + falling
    tile_rows = accumulated.shape[3]
    tile_cols = accumulated.shape[4]
    flattened = accumulated.reshape(own_count * NE * 2, 1, tile_rows, tile_cols)
    spread = lax.all_to_all(flattened, ("br", "bc"), split_axis=0, concat_axis=1, tiled=True)
    grid_rows = lax.axis_size("br")
    grid_cols = lax.axis_size("bc")
    per_device = spread.shape[0]
    tile_grid = spread.reshape(per_device, grid_rows, grid_cols, tile_rows, tile_cols)
    mirrored = jnp.swapaxes(tile_grid, 1, 2).reshape(spread.shape)
    device_number = lax.axis_index("br") * grid_cols + lax.axis_index("bc")
    item_number = device_number * per_device + jnp.arange(per_device, dtype=jnp.int32)
    parity = (item_number % 2).reshape(per_device, 1, 1, 1)
    signs = jnp.where(parity == 0, -1.0, 1.0).astype(jnp.float32)
    symmetric = (spread + signs * jnp.swapaxes(mirrored, -1, -2)) * 0.5
    returned = lax.all_to_all(symmetric, ("br", "bc"), split_axis=1, concat_axis=0, tiled=True)
    return returned.reshape(own_count, NE, 2, tile_rows, tile_cols)


def solution(mesh):
    in_specs = (
        P("ka", None, None, "br", "bc"),
        P(None, None, None, "br", "bc"),
        P(None, "ka", None),
    )
    out_specs = P("ka", None, None, "br", "bc")
    return jax.shard_map(
        on_device, mesh=mesh, in_specs=in_specs, out_specs=out_specs, check_vma=False
    )
```

profile of v0, /device:TPU:5, one launch (start us, length us, event | category | flops | bytes accessed | tf_op | source)
XLA Modules:
  0.0 139.2 jit_solution(8165242158302726737)
XLA Ops:
  0.0 1.3 broadcast_in_dim.7
  1.3 9.3 %all-to-all-start = ((s32[16,5,1,1]{1,3,2,0:T(1,128)}), s32[16,5,1,1]{1,3,2,0:T(1,128)S(1)}, u32[]{:S(2)}, u32[]{:S(2)}) async-start(s32[16,5,1,1]{1,3,2,0:T(1,128)} %broadcast_in_dim.7), calls=%async_computation | async-start | bytes 16384 | tf_op jit(solution)/shard_map/all_to_all | solution.py:11
  10.6 6.4 %slice_bitcast_fusion.7 = (f32[8,2,128,128]{3,2,1,0:T(8,128)S(1)}, f32[8,2,128,128]{3,2,1,0:T(8,128)S(1)}, f32[8,2,128,128]{3,2,1,0:T(8,128)S(1)}, f32[8,2,128,1...) fusion(f32[1,15,2,128,128]{4,3,2,1,0:T(8,128)} %param.3), kind=kLoop, calls=%fused_computation.24 | loop fusion | bytes 16777216 | tf_op jit(solution)/shard_map/squeeze | solution.py:37
  17.2 0.6 all-to-all-done
  17.9 0.6 constant_dynamic-slice_fusion.2
  20.9 0.6 constant_dynamic-slice_fusion
  26.6 3.2 %dynamic-slice_bitcast_fusion.4 = (f32[8,2,128,128]{3,2,1,0:T(8,128)S(1)}, f32[8,2,128,128]{3,2,1,0:T(8,128)S(1)}, f32[8,2,128,128]{3,2,1,0:T(8,128)S(1)}, f32[8...) fusion(f32[5,8,2,128,128]{4,3,2,1,0:T(8,128)} %param.4, s32[]{:T(128)S(6)} %select_n.58, s32[]{:T(128)S(6)} %select_n.64, ...), kind=kLoop, calls=%fused_computation.23 | loop fusion | bytes 10485780 | tf_op jit(solution)/shard_map/jit(dynamic_index_in_dim)/squeeze | solution.py:34
  29.9 0.3 copy-done.3
  30.3 0.3 copy-done.4
  30.6 1.1 add_subtract_fusion.3
  31.6 1.1 subtract_add_fusion.3
  32.8 1.1 add_subtract_fusion.2
  33.9 1.1 subtract_add_fusion.2
  35.1 1.1 add_subtract_fusion.1
  36.1 1.1 subtract_add_fusion.1
  37.3 3.0 %collective-permute-start.2 = (f32[1,8,2,128,128]{4,3,2,1,0:T(8,128)S(1)}, f32[1,8,2,128,128]{4,3,2,1,0:T(8,128)S(1)}, u32[]{:S(2)}, u32[]{:S(2)}) collective-permute-start(f32[1,8,2,128,128]{4,3,2,1,0:T(8,128)S(1)} %maximum_bitcast_fusion.3), channel_id=1, source_target_pairs={{0,240},{16,0},{32,16},{48,32},{64,48},{80,64},{96,80},{112,96},{1... | collective-permute-start | bytes 3145736 | tf_op jit(solution)/shard_map/ppermute | solution.py:27
  40.4 0.3 collective-permute-start
  40.7 1.1 subtract_add_fusion
  41.8 1.1 add_subtract_fusion
  42.9 18.7 %collective-permute-done.2 = f32[1,8,2,128,128]{4,3,2,1,0:T(8,128)S(1)} collective-permute-done((f32[1,8,2,128,128]{4,3,2,1,0:T(8,128)S(1)}, f32[1,8,2,128,128]{4,3,2,1,0:T(8,128)S(1)}, u32[]{:S(2)}, u32[]{:S(2)}) %collective-permute-start.2) | collective-permute-done | bytes 1048608 | tf_op jit(solution)/shard_map/ppermute | solution.py:27
  61.7 4.4 %collective-permute-start.3 = (f32[1,8,2,128,128]{4,3,2,1,0:T(8,128)S(1)}, f32[1,8,2,128,128]{4,3,2,1,0:T(8,128)S(1)}, u32[]{:S(2)}, u32[]{:S(2)}) collective-permute-start(f32[1,8,2,128,128]{4,3,2,1,0:T(8,128)S(1)} %fusion.3), channel_id=1, source_target_pairs={{0,240},{16,0},{32,16},{48,32},{64,48},{80,64},{96,80},{112,96},{1... | collective-permute-start | bytes 3145736 | tf_op jit(solution)/shard_map/ppermute | solution.py:27
  66.4 1.1 subtract_add_fusion.4
  67.5 1.1 add_subtract_fusion.4
  68.5 17.9 %collective-permute-done.3 = f32[1,8,2,128,128]{4,3,2,1,0:T(8,128)S(1)} collective-permute-done((f32[1,8,2,128,128]{4,3,2,1,0:T(8,128)S(1)}, f32[1,8,2,128,128]{4,3,2,1,0:T(8,128)S(1)}, u32[]{:S(2)}, u32[]{:S(2)}) %collective-permute-start.3) | collective-permute-done | bytes 1048608 | tf_op jit(solution)/shard_map/ppermute | solution.py:27
  86.5 4.2 %collective-permute-done.1 = f32[1,8,2,128,128]{4,3,2,1,0:T(8,128)S(1)} collective-permute-done((f32[1,8,2,128,128]{4,3,2,1,0:T(8,128)S(1)}, f32[1,8,2,128,128]{4,3,2,1,0:T(8,128)S(1)}, u32[]{:S(2)}, u32[]{:S(2)}) %collective-permute-start.1) | collective-permute-done | bytes 1048608 | tf_op jit(solution)/shard_map/ppermute | solution.py:27
  90.7 1.2 fusion.1
  91.9 10.0 %all-to-all-start.1 = ((f32[16,1,128,128]{3,2,1,0:T(8,128)}), f32[16,1,128,128]{3,2,1,0:T(8,128)S(1)}, u32[]{:S(2)}, u32[]{:S(2)}) async-start(f32[16,1,128,128]{3,2,1,0:T(8,128)} %bitcast.105), calls=%async_computation.1 | async-start | bytes 2097152 | tf_op jit(solution)/shard_map/all_to_all | solution.py:72
  101.9 15.3 %all-to-all-done.1 = f32[16,1,128,128]{3,2,1,0:T(8,128)S(1)} async-done(((f32[16,1,128,128]{3,2,1,0:T(8,128)}), f32[16,1,128,128]{3,2,1,0:T(8,128)S(1)}, u32[]{:S(2)}, u32[]{:S(2)}) %all-to-all-start.1) | async-done | bytes 1048608 | tf_op jit(solution)/shard_map/all_to_all | solution.py:72
  117.3 0.3 copy.5
  117.7 0.1 fusion.5
  117.8 20.4 %all_to_all.26 = f32[1,16,128,128]{3,2,0,1:T(8,128)S(1)} all-to-all(f32[1,16,128,128]{3,2,0,1:T(8,128)S(1)} %fusion.5), channel_id=1, replica_groups=mesh['ka'=16,'br'=4,'bc'=4] {'br','bc'}, dimensions={1} | all-to-all | bytes 2097152 | tf_op jit(solution)/shard_map/all_to_all | solution.py:83
  138.2 1.0 copy.8
  (23 shorter events, 1.2 us)
Async XLA Ops:
  1.3 16.5 %all-to-all-start = ((s32[16,5,1,1]{1,3,2,0:T(1,128)}), s32[16,5,1,1]{1,3,2,0:T(1,128)S(1)}, u32[]{:S(2)}, u32[]{:S(2)}) async-start(s32[16,5,1,1]{1,3,2,0:T(1,128)} %broadcast_in_dim.7), calls=%async_computation | async-start | bytes 16384 | tf_op jit(solution)/shard_map/all_to_all | solution.py:11
  10.6 6.4 %copy-start.5 = (s32[5,1,1]{0,2,1:T(1,128)S(1)}, s32[5,1,1]{0,2,1:T(1,128)}, u32[]{:S(2)}) copy-start(s32[5,1,1]{0,2,1:T(1,128)} %param.5) | copy-start | bytes 64
  26.5 3.4 %copy-start = (f32[8,2,128,128]{3,2,1,0:T(8,128)S(1)}, f32[8,2,128,128]{3,2,1,0:T(8,128)}, u32[]{:S(2)}) copy-start(f32[8,2,128,128]{3,2,1,0:T(8,128)} %get-tuple-element.13) | copy-start | bytes 3145732
  26.5 3.4 %copy-start.1 = (f32[8,2,128,128]{3,2,1,0:T(8,128)S(1)}, f32[8,2,128,128]{3,2,1,0:T(8,128)}, u32[]{:S(2)}) copy-start(f32[8,2,128,128]{3,2,1,0:T(8,128)} %get-tuple-element.14) | copy-start | bytes 3145732
  26.5 3.4 %copy-start.2 = (f32[8,2,128,128]{3,2,1,0:T(8,128)S(1)}, f32[8,2,128,128]{3,2,1,0:T(8,128)}, u32[]{:S(2)}) copy-start(f32[8,2,128,128]{3,2,1,0:T(8,128)} %get-tuple-element.15) | copy-start | bytes 3145732
  26.5 3.7 %copy-start.3 = (f32[8,2,128,128]{3,2,1,0:T(8,128)S(1)}, f32[8,2,128,128]{3,2,1,0:T(8,128)}, u32[]{:S(2)}) copy-start(f32[8,2,128,128]{3,2,1,0:T(8,128)} %get-tuple-element.16) | copy-start | bytes 3145732
  26.5 4.0 %copy-start.4 = (f32[8,2,128,128]{3,2,1,0:T(8,128)S(1)}, f32[8,2,128,128]{3,2,1,0:T(8,128)}, u32[]{:S(2)}) copy-start(f32[8,2,128,128]{3,2,1,0:T(8,128)} %get-tuple-element.17) | copy-start | bytes 3145732
  37.3 24.2 %collective-permute-start.2 = (f32[1,8,2,128,128]{4,3,2,1,0:T(8,128)S(1)}, f32[1,8,2,128,128]{4,3,2,1,0:T(8,128)S(1)}, u32[]{:S(2)}, u32[]{:S(2)}) collective-permute-start(f32[1,8,2,128,128]{4,3,2,1,0:T(8,128)S(1)} %maximum_bitcast_fusion.3), channel_id=1, source_target_pairs={{0,240},{16,0},{32,16},{48,32},{64,48},{80,64},{96,80},{112,96},{1... | collective-permute-start | bytes 3145736 | tf_op jit(solution)/shard_map/ppermute | solution.py:27
  40.4 25.7 %collective-permute-start = (f32[1,8,2,128,128]{4,3,2,1,0:T(8,128)S(1)}, f32[1,8,2,128,128]{4,3,2,1,0:T(8,128)S(1)}, u32[]{:S(2)}, u32[]{:S(2)}) collective-permute-start(f32[1,8,2,128,128]{4,3,2,1,0:T(8,128)S(1)} %maximum_bitcast_fusion.1), channel_id=1, source_target_pairs={{0,16},{16,32},{32,48},{48,64},{64,80},{80,96},{96,112},{112,128},... | collective-permute-start | bytes 3145736 | tf_op jit(solution)/shard_map/ppermute | solution.py:27
  61.7 24.8 %collective-permute-start.3 = (f32[1,8,2,128,128]{4,3,2,1,0:T(8,128)S(1)}, f32[1,8,2,128,128]{4,3,2,1,0:T(8,128)S(1)}, u32[]{:S(2)}, u32[]{:S(2)}) collective-permute-start(f32[1,8,2,128,128]{4,3,2,1,0:T(8,128)S(1)} %fusion.3), channel_id=1, source_target_pairs={{0,240},{16,0},{32,16},{48,32},{64,48},{80,64},{96,80},{112,96},{1... | collective-permute-start | bytes 3145736 | tf_op jit(solution)/shard_map/ppermute | solution.py:27
  66.2 24.5 %collective-permute-start.1 = (f32[1,8,2,128,128]{4,3,2,1,0:T(8,128)S(1)}, f32[1,8,2,128,128]{4,3,2,1,0:T(8,128)S(1)}, u32[]{:S(2)}, u32[]{:S(2)}) collective-permute-start(f32[1,8,2,128,128]{4,3,2,1,0:T(8,128)S(1)} %fusion.2), channel_id=1, source_target_pairs={{0,16},{16,32},{32,48},{48,64},{64,80},{80,96},{96,112},{112,128},... | collective-permute-start | bytes 3145736 | tf_op jit(solution)/shard_map/ppermute | solution.py:27
  91.9 25.3 %all-to-all-start.1 = ((f32[16,1,128,128]{3,2,1,0:T(8,128)}), f32[16,1,128,128]{3,2,1,0:T(8,128)S(1)}, u32[]{:S(2)}, u32[]{:S(2)}) async-start(f32[16,1,128,128]{3,2,1,0:T(8,128)} %bitcast.105), calls=%async_computation.1 | async-start | bytes 2097152 | tf_op jit(solution)/shard_map/all_to_all | solution.py:72
where the time goes:
time: 141 us; the launch traced here: 139 us
  waiting for transfers between devices  56.7 us (40%)
  starting transfers between devices  27 us (19%)
  blocking collectives  20.4 us (14%)
  local copies, waits for them, and re-layouts  14.6 us (10%)
  other arithmetic  12.5 us (9%)
  between operations  7.88 us (6%)
    ppermute x4, waiting for transfers between devices, shifted(): return lax.ppermute(x, axis, [(i, (i + by) % size) for i in range(size)])  40.8 us
    all_to_all x1, blocking collectives, on_device(): lax.all_to_all(symmetric, ('br', 'bc'), split_axis=1, concat_axis=0, tile...  20.4 us
    all_to_all x1, waiting for transfers between devices, on_device(): lax.all_to_all(flattened, ('br', 'bc'), split_axis=0, concat_axis=1, tile...  15.3 us
    all_to_all x1, starting transfers between devices, on_device(): lax.all_to_all(flattened, ('br', 'bc'), split_axis=0, concat_axis=1, tile...  9.99 us
    all_to_all x1, starting transfers between devices, sent_to_all(): return lax.all_to_all(copies, axis, split_axis=0, concat_axis=0, tiled=True)  9.3 us
    ppermute x4, starting transfers between devices, shifted(): return lax.ppermute(x, axis, [(i, (i + by) % size) for i in range(size)])  7.69 us
    squeeze x1, local copies, waits for them, and re-layouts, stop_terms(): window = remote[0, lag_start:lag_start + energies]  6.42 us
    add x5, other arithmetic, stop_terms(): imag_sum = imag_sum + (green_real * inter_real - green_imag * inter_imag)  5.37 us
  transfers between devices with their start and end apart: 6, of which 5 were waited for; matrix products, arithmetic and copies ran while one was open for 8% of the time, Pallas kernels for 0%

commit v1 on v0

v1 whole, which is shorter than its diff:
```python
import functools

import jax
import jax.numpy as jnp
from jax import lax
from jax.experimental import pallas as pl
from jax.experimental.pallas import tpu as pltpu
from jax.sharding import PartitionSpec as P

NE = 8
NW = 8
GROUP = 2
MESH = pl.DeviceIdType.MESH
FAR_UP, FAR_DOWN, NEAR_UP, NEAR_DOWN = range(4)
HOPS = (2, -2, 1, -1)
STOPS = (3, 4, 1, 2)
STEPS = (1, -1, 1, -1)


def kernel(
    sizes, green_hbm, screened_hbm, table, out_hbm,
    green, screened, tables, src, rcv, give, take, total, mirror, result, work,
    load_sem, table_send, table_recv, ring_send, ring_recv, pair_send, pair_recv,
    mirror_send, mirror_recv, out_sem,
):
    n_ka = sizes["ka"]
    k, r, c = lax.axis_index("ka"), lax.axis_index("br"), lax.axis_index("bc")
    is_diag = r == c
    is_near = (r // GROUP == c // GROUP) & (r != c)
    is_far = r // GROUP != c // GROUP
    partner = (k, c, r)

    def at_hop(hop):
        return (lax.rem(k + hop + n_ka, n_ka), r, c)

    barrier = pltpu.get_barrier_semaphore()
    for hop in HOPS:
        pl.semaphore_signal(barrier, inc=1, device_id=at_hop(hop), device_id_type=MESH)

    @pl.when(jnp.logical_not(is_diag))
    def _():
        pl.semaphore_signal(barrier, inc=1, device_id=partner, device_id_type=MESH)

    loads = [
        pltpu.make_async_copy(green_hbm.at[0], green, load_sem.at[0]),
        pltpu.make_async_copy(screened_hbm, screened, load_sem.at[1]),
    ]
    for load in loads:
        load.start()

    @pl.when(is_diag)
    def _():
        pl.semaphore_wait(barrier, len(HOPS))

    @pl.when(jnp.logical_not(is_diag))
    def _():
        pl.semaphore_wait(barrier, len(HOPS) + 1)

    def table_copy(i):
        return pltpu.make_async_remote_copy(
            src_ref=table, dst_ref=tables.at[i], send_sem=table_send.at[i], recv_sem=table_recv.at[i],
            device_id=at_hop(-HOPS[i]), device_id_type=MESH,
        )

    for i in range(4):
        table_copy(i).start()
    for load in loads:
        load.wait()
    for i in range(4):
        table_copy(i).wait_recv()
    slots = [tables[i, STOPS[i], 0] for i in range(4)]
    own_slot = table[0, 0]

    def ring_copy(d, j):
        return pltpu.make_async_remote_copy(
            src_ref=src.at[d, j], dst_ref=rcv.at[d, j], send_sem=ring_send.at[d, j], recv_sem=ring_recv.at[d, j],
            device_id=at_hop(STEPS[d]), device_id_type=MESH,
        )

    def pair_copy(d, j):
        return pltpu.make_async_remote_copy(
            src_ref=give.at[d, j], dst_ref=take.at[d, j], send_sem=pair_send.at[d, j], recv_sem=pair_recv.at[d, j],
            device_id=partner, device_id_type=MESH,
        )

    def mirror_copy(e):
        return pltpu.make_async_remote_copy(
            src_ref=total.at[e], dst_ref=mirror.at[e], send_sem=mirror_send.at[e], recv_sem=mirror_recv.at[e],
            device_id=partner, device_id_type=MESH,
        )

    def out_copy(e):
        return pltpu.make_async_copy(result.at[e], out_hbm.at[0, e], out_sem.at[e])

    tile_rows = green.shape[2]

    def terms(dsts, slot, first, added=None):
        count = len(dsts)

        def block(i, carry):
            rows = pl.ds(pl.multiple_of(i * 8, 8), 8)
            real, imag = [None] * count, [None] * count
            window = [[green[first + lag, part, rows, :] for part in range(2)] for lag in range(count + NW - 1)]
            for w in range(NW):
                wr, wi = screened[slot, w, 0, rows, :], screened[slot, w, 1, rows, :]
                for n in range(count):
                    gr, gi = window[n + NW - 1 - w]
                    plus, minus = gr * wi + gi * wr, gr * wr - gi * wi
                    real[n] = -plus if w == 0 else real[n] - plus
                    imag[n] = minus if w == 0 else imag[n] + minus
            for n in range(count):
                if added is not None:
                    real[n] = real[n] + added[0, rows, :]
                    imag[n] = imag[n] + added[1, rows, :]
                dsts[n][0, rows, :] = real[n]
                dsts[n][1, rows, :] = imag[n]
            return carry

        lax.fori_loop(0, tile_rows // 8, block, 0)

    def write_out(e, other):
        result[e, 0] = (total[e, 0] - other[e, 0].T) * 0.5
        result[e, 1] = (total[e, 1] + other[e, 1].T) * 0.5
        out_copy(e).start()

    def each(count, body):
        def step(i, carry):
            body(i)
            return carry

        lax.fori_loop(0, count, step, 0)

    def own_terms(i):
        terms([total.at[2 * i], total.at[2 * i + 1]], own_slot, 2 * i)

    @pl.when(is_far)
    def _():
        def step(i):
            @pl.when(i < NE)
            def _():
                for d in (FAR_UP, FAR_DOWN):
                    terms([src.at[d, i]], slots[d], i)
                    ring_copy(d, i).start()

            @pl.when((i >= 2) & (i < NE + 2))
            def _():
                for d in (NEAR_UP, NEAR_DOWN):
                    ring_copy(d - 2, i - 2).wait_recv()
                    terms([src.at[d, i - 2]], slots[d], i - 2, rcv.at[d - 2, i - 2])
                    ring_copy(d, i - 2).start()

            @pl.when(i < NE)
            def _():
                terms([total.at[i]], own_slot, i)

            @pl.when((i >= 4) & (i < NE + 4))
            def _():
                e = i - 4
                for d in (NEAR_UP, NEAR_DOWN):
                    ring_copy(d, e).wait_recv()
                total[e] = total[e] + (rcv[NEAR_UP, e] + rcv[NEAR_DOWN, e])
                mirror_copy(e).start()

            @pl.when(i >= 5)
            def _():
                e = i - 5
                mirror_copy(e).wait_recv()
                write_out(e, mirror)

        each(NE + 5, step)

        def close(e):
            for d in range(4):
                ring_copy(d, e).wait_send()
            mirror_copy(e).wait_send()

        each(NE, close)

    half = NE // 2

    @pl.when(is_near)
    def _():
        mine = jnp.where(r < c, 0, half)
        theirs = half - mine

        def offer(i):
            for d in range(4):
                terms([give.at[d, i]], slots[d], theirs + i)
                pair_copy(d, i).start()

        def joined(d, j, added):
            terms([work.at[0]], slots[d], mine + j, added)
            pair_copy(d, j).wait_recv()
            src[d, j, 0] = work[0, 0] - take[d, j, 0].T
            src[d, j, 1] = work[0, 1] + take[d, j, 1].T
            ring_copy(d, j).start()

        def step(i):
            @pl.when(i < half)
            def _():
                offer(i)

            @pl.when((i >= 1) & (i < half + 1))
            def _():
                for d in (FAR_UP, FAR_DOWN):
                    joined(d, i - 1, None)

            @pl.when(i < half)
            def _():
                own_terms(i)

            @pl.when((i >= 2) & (i < half + 2))
            def _():
                for d in (NEAR_UP, NEAR_DOWN):
                    ring_copy(d - 2, i - 2).wait_recv()
                    joined(d, i - 2, rcv.at[d - 2, i - 2])

            @pl.when(i == half)
            def _():
                each(half, lambda j: mirror_copy(theirs + j).start())

            @pl.when(i >= 3)
            def _():
                j = i - 3
                e = mine + j
                for d in (NEAR_UP, NEAR_DOWN):
                    ring_copy(d, j).wait_recv()
                total[e] = total[e] + (rcv[NEAR_UP, j] + rcv[NEAR_DOWN, j])

            @pl.when(i == half)
            def _():
                for j in range(2):
                    mirror_copy(mine + j).start()

            @pl.when(i > half)
            def _():
                mirror_copy(mine + i - 3).start()

        each(half + 3, step)

        def finish(j):
            for first in (mine, theirs):
                mirror_copy(first + j).wait_recv()
                write_out(first + j, mirror)

        each(half, finish)

        def close(j):
            for d in range(4):
                ring_copy(d, j).wait_send()
                pair_copy(d, j).wait_send()
            mirror_copy(j).wait_send()
            mirror_copy(half + j).wait_send()

        each(half, close)

    @pl.when(is_diag)
    def _():
        row = lax.broadcasted_iota(jnp.int32, (tile_rows, tile_rows), 0)
        col = lax.broadcasted_iota(jnp.int32, (tile_rows, tile_rows), 1)

        def folded(d, j, added):
            terms([work.at[0], work.at[1]], slots[d], 2 * j)
            real = [work[n, 0] - work[n, 0].T for n in range(2)]
            imag = [work[n, 1] + work[n, 1].T for n in range(2)]
            packed_real = jnp.where(row < col, real[0], jnp.where(row > col, real[1], imag[1]))
            packed_imag = jnp.where(row <= col, imag[0], imag[1])
            if added is not None:
                packed_real, packed_imag = packed_real + added[0], packed_imag + added[1]
            src[d, j, 0] = packed_real
            src[d, j, 1] = packed_imag
            ring_copy(d, j).start()

        def step(i):
            @pl.when(i < half)
            def _():
                for d in (FAR_UP, FAR_DOWN):
                    folded(d, i, None)

            @pl.when((i >= 1) & (i < half + 1))
            def _():
                for d in (NEAR_UP, NEAR_DOWN):
                    ring_copy(d - 2, i - 1).wait_recv()
                    folded(d, i - 1, rcv.at[d - 2, i - 1])

            @pl.when(i < half)
            def _():
                own_terms(i)

            @pl.when(i >= 2)
            def _():
                j = i - 2
                for d in (NEAR_UP, NEAR_DOWN):
                    ring_copy(d, j).wait_recv()
                real = rcv[NEAR_UP, j, 0] + rcv[NEAR_DOWN, j, 0]
                imag = rcv[NEAR_UP, j, 1] + rcv[NEAR_DOWN, j, 1]
                zero = jnp.zeros_like(real)
                total[2 * j, 0] = total[2 * j, 0] + jnp.where(row < col, real, zero)
                total[2 * j, 1] = total[2 * j, 1] + jnp.where(row < col, imag, jnp.where(row == col, imag * 0.5, zero))
                total[2 * j + 1, 0] = total[2 * j + 1, 0] + jnp.where(row > col, real, zero)
                total[2 * j + 1, 1] = total[2 * j + 1, 1] + jnp.where(row > col, imag, jnp.where(row == col, real * 0.5, zero))
                for n in range(2):
                    write_out(2 * j + n, total)

        each(half + 2, step)

        def close(j):
            for d in range(4):
                ring_copy(d, j).wait_send()

        each(half, close)

    for i in range(4):
        table_copy(i).wait_send()
    each(NE, lambda e: out_copy(e).wait())


def solution(mesh):
    sizes = dict(mesh.shape)

    def on_device(green_lesser, screened, slot_table):
        _, lags, _, rows, cols = green_lesser.shape
        tile = (2, rows, cols)
        half = NE // 2
        f32, dma = jnp.float32, pltpu.SemaphoreType.DMA
        anywhere = pl.BlockSpec(memory_space=pl.ANY)
        return pl.pallas_call(
            functools.partial(kernel, sizes),
            out_shape=jax.ShapeDtypeStruct((1, NE, *tile), f32),
            in_specs=[anywhere, anywhere, pl.BlockSpec(memory_space=pltpu.SMEM)],
            out_specs=anywhere,
            scratch_shapes=[
                pltpu.VMEM((lags, *tile), f32),
                pltpu.VMEM(screened.shape, f32),
                pltpu.SMEM((4, slot_table.shape[0], 1), jnp.int32),
                pltpu.VMEM((4, NE, *tile), f32),
                pltpu.VMEM((4, NE, *tile), f32),
                pltpu.VMEM((4, half, *tile), f32),
                pltpu.VMEM((4, half, *tile), f32),
                pltpu.VMEM((NE, *tile), f32),
                pltpu.VMEM((NE, *tile), f32),
                pltpu.VMEM((NE, *tile), f32),
                pltpu.VMEM((2, *tile), f32),
                dma((2,)),
                dma((4,)),
                dma((4,)),
                dma((4, NE)),
                dma((4, NE)),
                dma((4, half)),
                dma((4, half)),
                dma((NE,)),
                dma((NE,)),
                dma((NE,)),
            ],
            compiler_params=pltpu.CompilerParams(
                collective_id=0, has_side_effects=True, vmem_limit_bytes=48 * 1024 * 1024
            ),
            name="self_energy",
        )(green_lesser, screened, slot_table.reshape(slot_table.shape[0], 1))

    in_specs = (
        P("ka", None, None, "br", "bc"),
        P(None, None, None, "br", "bc"),
        P(None, "ka", None),
    )
    out_specs = P("ka", None, None, "br", "bc")
    return jax.shard_map(on_device, mesh=mesh, in_specs=in_specs, out_specs=out_specs, check_vma=False)
```

time: 141 us -> 73.8 us (0.52); the launches traced: 139 us -> 73.4 us
  Pallas kernels: 0 us -> 70.1 us
  waiting for transfers between devices: 56.7 us -> 0 us
  starting transfers between devices: 27 us -> 0 us
  blocking collectives: 20.4 us -> 0 us
  other arithmetic: 12.5 us -> 0 us
  local copies, waits for them, and re-layouts: 14.6 us -> 3.26 us
  between operations: 7.88 us -> 0.01 us
    pallas_call x0 -> x1, Pallas kernels: none -> 70.1 us  [on_device(): pl.pallas_call(functools.partial(kernel, sizes), out_shape=jax.ShapeDtype...]
    ppermute x4 -> x0, waiting for transfers between devices: 40.8 us -> none  [shifted(): return lax.ppermute(x, axis, [(i, (i + by) % size) for i in range(size)])]
    all_to_all x1 -> x0, blocking collectives: 20.4 us -> none  [on_device(): lax.all_to_all(symmetric, ('br', 'bc'), split_axis=1, concat_axis=0, tile...]
    all_to_all x2 -> x0, starting transfers between devices: 19.3 us -> none  [the longest x1 9.99 us: on_device(): lax.all_to_all(flattened, ('br', 'bc'), split_axis=0, concat_axis=1, tile...]
    all_to_all x2 -> x0, waiting for transfers between devices: 15.9 us -> none  [the longest x1 15.3 us: on_device(): lax.all_to_all(flattened, ('br', 'bc'), split_axis=0, concat_axis=1, tile...]
    squeeze x2 -> x0, local copies, waits for them, and re-layouts: 9.66 us -> none  [the longest x1 6.42 us: stop_terms(): window = remote[0, lag_start:lag_start + energies]]
    ppermute x4 -> x0, starting transfers between devices: 7.69 us -> none  [shifted(): return lax.ppermute(x, axis, [(i, (i + by) % size) for i in range(size)])]
    add x8 -> x0, other arithmetic: 6.79 us -> none  [the longest x5 5.37 us: stop_terms(): imag_sum = imag_sum + (green_real * inter_real - green_imag * inter_imag)]
  transfers between devices with their start and end apart: 6 -> 0, of which waited for: 5 -> 0; matrix products, arithmetic and copies ran while one was open for 8% -> 0% of each run, Pallas kernels for 0% -> 0%
where the time goes in v1:
time: 73.8 us; the launch traced here: 73.4 us
  Pallas kernels  70.1 us (95%)
  local copies, waits for them, and re-layouts  3.26 us (4%)
    pallas_call x1, Pallas kernels, on_device(): pl.pallas_call(functools.partial(kernel, sizes), out_shape=jax.ShapeDtype...  70.1 us
    unnamed x3, local copies, waits for them, and re-layouts  2.52 us

profile of v1, /device:TPU:5, one launch (start us, length us, event | category | flops | bytes accessed | tf_op | source)
XLA Modules:
  0.0 73.4 jit_solution(7140055667015636800)
XLA Ops:
  0.0 0.7 %copy.4.table = s32[5,1]{1,0:T(8,128)S(1)} copy(s32[5,1]{0,1:T(1,128)} %bitcast.1) | data formatting | bytes 40 | tf_op jit(solution)/shard_map/reshape | solution.py:359
  0.7 0.0 copy-start
  0.7 1.5 %copy-done = f32[1,15,2,128,128]{4,3,2,1,0:T(8,128)S(1)} copy-done((f32[1,15,2,128,128]{4,3,2,1,0:T(8,128)S(1)}, f32[1,15,2,128,128]{4,3,2,1,0:T(8,128)}, u32[]{:S(2)}) %copy-start) | copy-done | bytes 1966104
  2.3 70.1 %self_energy.1 = f32[1,8,2,128,128]{4,3,2,1,0:T(8,128)S(1)} custom-call(f32[1,15,2,128,128]{4,3,2,1,0:T(8,128)S(1)} %copy-done, f32[5,8,2,128,128]{4,3,2,1,0:T(8,128)} %screened_hbm.1, s32[5,1]{1,0:T(8,128)S(1)} %copy.4.table), custom_call_target="tpu_custom_call" | custom-call | tf_op jit(solution)/shard_map/self_energy/pallas_call | solution.py:327
  72.4 1.0 %copy.6 = f32[1,8,2,128,128]{4,3,2,1,0:T(8,128)} copy(f32[1,8,2,128,128]{4,3,2,1,0:T(8,128)S(1)} %self_energy.1) | data formatting | bytes 2097152
Async XLA Ops:
  0.7 1.5 %copy-start = (f32[1,15,2,128,128]{4,3,2,1,0:T(8,128)S(1)}, f32[1,15,2,128,128]{4,3,2,1,0:T(8,128)}, u32[]{:S(2)}) copy-start(f32[1,15,2,128,128]{4,3,2,1,0:T(8,128)} %green_hbm.1) | copy-start | bytes 5898244

commit v2 on v1

--- a/solution.py
+++ b/solution.py
@@ -18,8 +18,8 @@
 
 
 def kernel(
-    sizes, green_hbm, screened_hbm, table, out_hbm,
-    green, screened, tables, src, rcv, give, take, total, mirror, result, work,
+    sizes, green_hbm, screened_hbm, table_hbm, out_hbm,
+    table, green, screened, tables, src, rcv, give, take, total, mirror, result, work,
     load_sem, table_send, table_recv, ring_send, ring_recv, pair_send, pair_recv,
     mirror_send, mirror_recv, out_sem,
 ):
@@ -44,6 +44,7 @@
     loads = [
         pltpu.make_async_copy(green_hbm.at[0], green, load_sem.at[0]),
         pltpu.make_async_copy(screened_hbm, screened, load_sem.at[1]),
+        pltpu.make_async_copy(table_hbm, table, load_sem.at[2]),
     ]
     for load in loads:
         load.start()
@@ -62,43 +63,18 @@
             device_id=at_hop(-HOPS[i]), device_id_type=MESH,
         )
 
+    loads[2].wait()
     for i in range(4):
         table_copy(i).start()
-    for load in loads:
+    for load in loads[:2]:
         load.wait()
-    for i in range(4):
-        table_copy(i).wait_recv()
-    slots = [tables[i, STOPS[i], 0] for i in range(4)]
-    own_slot = table[0, 0]
-
-    def ring_copy(d, j):
-        return pltpu.make_async_remote_copy(
-            src_ref=src.at[d, j], dst_ref=rcv.at[d, j], send_sem=ring_send.at[d, j], recv_sem=ring_recv.at[d, j],
-            device_id=at_hop(STEPS[d]), device_id_type=MESH,
-        )
-
-    def pair_copy(d, j):
-        return pltpu.make_async_remote_copy(
-            src_ref=give.at[d, j], dst_ref=take.at[d, j], send_sem=pair_send.at[d, j], recv_sem=pair_recv.at[d, j],
-            device_id=partner, device_id_type=MESH,
-        )
-
-    def mirror_copy(e):
-        return pltpu.make_async_remote_copy(
-            src_ref=total.at[e], dst_ref=mirror.at[e], send_sem=mirror_send.at[e], recv_sem=mirror_recv.at[e],
-            device_id=partner, device_id_type=MESH,
-        )
-
-    def out_copy(e):
-        return pltpu.make_async_copy(result.at[e], out_hbm.at[0, e], out_sem.at[e])
-
     tile_rows = green.shape[2]
 
-    def terms(dsts, slot, first, added=None):
+    def terms(dsts, slot, first, added=None, start=0, size=tile_rows):
         count = len(dsts)
 
         def block(i, carry):
-            rows = pl.ds(pl.multiple_of(i * 8, 8), 8)
+            rows = pl.ds(pl.multiple_of(start + i * 8, 8), 8)
             real, imag = [None] * count, [None] * count
             window = [[green[first + lag, part, rows, :] for part in range(2)] for lag in range(count + NW - 1)]
             for w in range(NW):
@@ -116,65 +92,115 @@
                 dsts[n][1, rows, :] = imag[n]
             return carry
 
-        lax.fori_loop(0, tile_rows // 8, block, 0)
+        lax.fori_loop(0, size // 8, block, 0)
+
+    def each(count, body):
+        def step(i, carry):
+            body(i)
+            return carry
+
+        lax.fori_loop(0, count, step, 0)
+
+    def own_terms(i):
+        terms([total.at[2 * i], total.at[2 * i + 1]], table[0, 0, 0], 2 * i)
+
+    each(NE // 2, own_terms)
+    for i in range(4):
+        table_copy(i).wait_recv()
+    slots = [tables[i, 0, 0, STOPS[i]] for i in range(4)]
+
+    def ring_copy(d, j):
+        return pltpu.make_async_remote_copy(
+            src_ref=src.at[d, j], dst_ref=rcv.at[d, j], send_sem=ring_send.at[d, j], recv_sem=ring_recv.at[d, j],
+            device_id=at_hop(STEPS[d]), device_id_type=MESH,
+        )
+
+    def pair_copy(d, j):
+        return pltpu.make_async_remote_copy(
+            src_ref=give.at[d, j], dst_ref=take.at[d, j], send_sem=pair_send.at[d, j], recv_sem=pair_recv.at[d, j],
+            device_id=partner, device_id_type=MESH,
+        )
+
+    def mirror_copy(e):
+        return pltpu.make_async_remote_copy(
+            src_ref=total.at[e], dst_ref=mirror.at[e], send_sem=mirror_send.at[e], recv_sem=mirror_recv.at[e],
+            device_id=partner, device_id_type=MESH,
+        )
+
+    def out_copy(e):
+        return pltpu.make_async_copy(result.at[e], out_hbm.at[0, e], out_sem.at[e])
 
     def write_out(e, other):
         result[e, 0] = (total[e, 0] - other[e, 0].T) * 0.5
         result[e, 1] = (total[e, 1] + other[e, 1].T) * 0.5
         out_copy(e).start()
 
-    def each(count, body):
-        def step(i, carry):
-            body(i)
-            return carry
-
-        lax.fori_loop(0, count, step, 0)
-
-    def own_terms(i):
-        terms([total.at[2 * i], total.at[2 * i + 1]], own_slot, 2 * i)
-
     @pl.when(is_far)
     def _():
+        piece = tile_rows // 2
+        pieces = 2 * NE
+
+        def at(u):
+            return lax.div(u, 2), pl.multiple_of(lax.rem(u, 2) * piece, piece)
+
+        def ring_piece(d, u):
+            e, start = at(u)
+            return pltpu.make_async_remote_copy(
+                src_ref=src.at[d, e, :, pl.ds(start, piece)], dst_ref=rcv.at[d, e, :, pl.ds(start, piece)],
+                send_sem=ring_send.at[d, u], recv_sem=ring_recv.at[d, u],
+                device_id=at_hop(STEPS[d]), device_id_type=MESH,
+            )
+
+        def mirror_piece(u):
+            e, start = at(u)
+            return pltpu.make_async_remote_copy(
+                src_ref=total.at[e, :, pl.ds(start, piece)], dst_ref=mirror.at[e, :, pl.ds(start, piece)],
+                send_sem=mirror_send.at[u], recv_sem=mirror_recv.at[u],
+                device_id=partner, device_id_type=MESH,
+            )
+
         def step(i):
-            @pl.when(i < NE)
-            def _():
+            @pl.when(i < pieces)
+            def _():
+                e, start = at(i)
                 for d in (FAR_UP, FAR_DOWN):
-                    terms([src.at[d, i]], slots[d], i)
-                    ring_copy(d, i).start()
-
-            @pl.when((i >= 2) & (i < NE + 2))
-            def _():
-                for d in (NEAR_UP, NEAR_DOWN):
-                    ring_copy(d - 2, i - 2).wait_recv()
-                    terms([src.at[d, i - 2]], slots[d], i - 2, rcv.at[d - 2, i - 2])
-                    ring_copy(d, i - 2).start()
-
-            @pl.when(i < NE)
-            def _():
-                terms([total.at[i]], own_slot, i)
-
-            @pl.when((i >= 4) & (i < NE + 4))
-            def _():
-                e = i - 4
-                for d in (NEAR_UP, NEAR_DOWN):
-                    ring_copy(d, e).wait_recv()
-                total[e] = total[e] + (rcv[NEAR_UP, e] + rcv[NEAR_DOWN, e])
-                mirror_copy(e).start()
-
-            @pl.when(i >= 5)
-            def _():
-                e = i - 5
-                mirror_copy(e).wait_recv()
+                    terms([src.at[d, e]], slots[d], e, None, start, piece)
+                    ring_piece(d, i).start()
+
+            @pl.when((i >= 3) & (i < pieces + 3))
+            def _():
+                u = i - 3
+                e, start = at(u)
+                for d in (NEAR_UP, NEAR_DOWN):
+                    ring_piece(d - 2, u).wait_recv()
+                    terms([src.at[d, e]], slots[d], e, rcv.at[d - 2, e], start, piece)
+                    ring_piece(d, u).start()
+
+            @pl.when((i >= 6) & (i < pieces + 6))
+            def _():
+                u = i - 6
+                e, start = at(u)
+                rows = pl.ds(start, piece)
+                for d in (NEAR_UP, NEAR_DOWN):
+                    ring_piece(d, u).wait_recv()
+                total[e, :, rows] = total[e, :, rows] + (rcv[NEAR_UP, e, :, rows] + rcv[NEAR_DOWN, e, :, rows])
+                mirror_piece(u).start()
+
+            @pl.when((i >= 10) & (lax.rem(i, 2) == 0))
+            def _():
+                e = lax.div(i - 10, 2)
+                for n in range(2):
+                    mirror_piece(2 * e + n).wait_recv()
                 write_out(e, mirror)
 
-        each(NE + 5, step)
-
-        def close(e):
+        each(pieces + 9, step)
+
+        def close(u):
             for d in range(4):
-                ring_copy(d, e).wait_send()
-            mirror_copy(e).wait_send()
-
-        each(NE, close)
+                ring_piece(d, u).wait_send()
+            mirror_piece(u).wait_send()
+
+        each(pieces, close)
 
     half = NE // 2
 
@@ -204,10 +230,6 @@
             def _():
                 for d in (FAR_UP, FAR_DOWN):
                     joined(d, i - 1, None)
-
-            @pl.when(i < half)
-            def _():
-                own_terms(i)
 
             @pl.when((i >= 2) & (i < half + 2))
             def _():
@@ -283,10 +305,6 @@
                     ring_copy(d - 2, i - 1).wait_recv()
                     folded(d, i - 1, rcv.at[d - 2, i - 1])
 
-            @pl.when(i < half)
-            def _():
-                own_terms(i)
-
             @pl.when(i >= 2)
             def _():
                 j = i - 2
@@ -323,16 +341,17 @@
         tile = (2, rows, cols)
         half = NE // 2
         f32, dma = jnp.float32, pltpu.SemaphoreType.DMA
-        anywhere = pl.BlockSpec(memory_space=pl.ANY)
+        in_hbm = pl.BlockSpec(memory_space=pltpu.HBM)
         return pl.pallas_call(
             functools.partial(kernel, sizes),
             out_shape=jax.ShapeDtypeStruct((1, NE, *tile), f32),
-            in_specs=[anywhere, anywhere, pl.BlockSpec(memory_space=pltpu.SMEM)],
-            out_specs=anywhere,
+            in_specs=[in_hbm, in_hbm, in_hbm],
+            out_specs=in_hbm,
             scratch_shapes=[
+                pltpu.SMEM((1, 1, slot_table.shape[0]), jnp.int32),
                 pltpu.VMEM((lags, *tile), f32),
                 pltpu.VMEM(screened.shape, f32),
-                pltpu.SMEM((4, slot_table.shape[0], 1), jnp.int32),
+                pltpu.SMEM((4, 1, 1, slot_table.shape[0]), jnp.int32),
                 pltpu.VMEM((4, NE, *tile), f32),
                 pltpu.VMEM((4, NE, *tile), f32),
                 pltpu.VMEM((4, half, *tile), f32),
@@ -341,22 +360,22 @@
                 pltpu.VMEM((NE, *tile), f32),
                 pltpu.VMEM((NE, *tile), f32),
                 pltpu.VMEM((2, *tile), f32),
-                dma((2,)),
+                dma((3,)),
                 dma((4,)),
                 dma((4,)),
-                dma((4, NE)),
-                dma((4, NE)),
+                dma((4, 2 * NE)),
+                dma((4, 2 * NE)),
                 dma((4, half)),
                 dma((4, half)),
-                dma((NE,)),
-                dma((NE,)),
+                dma((2 * NE,)),
+                dma((2 * NE,)),
                 dma((NE,)),
             ],
             compiler_params=pltpu.CompilerParams(
-                collective_id=0, has_side_effects=True, vmem_limit_bytes=48 * 1024 * 1024
+                collective_id=0, has_side_effects=True, vmem_limit_bytes=66_000_000
             ),
             name="self_energy",
-        )(green_lesser, screened, slot_table.reshape(slot_table.shape[0], 1))
+        )(green_lesser, screened, slot_table.transpose(1, 2, 0))
 
     in_specs = (
         P("ka", None, None, "br", "bc"),

time: 73.8 us -> 70.9 us (0.961)
  Pallas kernels: 70.1 us -> 68.5 us
  local copies, waits for them, and re-layouts: 3.26 us -> 2.3 us
    pallas_call x1, Pallas kernels: 70.1 us -> 68.5 us  [on_device(): pl.pallas_call(functools.partial(kernel, sizes), out_shape=jax.ShapeDtype...]
    reshape x1 -> x0, local copies, waits for them, and re-layouts: 0.74 us -> none  [on_device(): slot_table.reshape(slot_table.shape[0], 1)]
    unnamed x3 -> x1, local copies, waits for them, and re-layouts: 2.52 us -> 2.3 us
where the time goes in v2:
time: 70.9 us; the launch traced here: 70.8 us
  Pallas kernels  68.5 us (97%)
  local copies, waits for them, and re-layouts  2.3 us (3%)
    pallas_call x1, Pallas kernels, on_device(): pl.pallas_call(functools.partial(kernel, sizes), out_shape=jax.ShapeDtype...  68.5 us
    unnamed x1, local copies, waits for them, and re-layouts  2.3 us

profile of v2, /device:TPU:5, one launch (start us, length us, event | category | flops | bytes accessed | tf_op | source)
XLA Modules:
  0.0 70.8 jit_solution(4335782502447803702)
XLA Ops:
  0.0 68.5 %self_energy.1 = f32[1,8,2,128,128]{4,3,2,1,0:T(8,128)} custom-call(f32[1,15,2,128,128]{4,3,2,1,0:T(8,128)} %green_hbm.1, f32[5,8,2,128,128]{4,3,2,1,0:T(8,128)} %screened_hbm.1, s32[1,1,5]{2,1,0:T(1,128)} %bitcast.1), custom_call_target="tpu_custom_call" | custom-call | tf_op jit(solution)/shard_map/self_energy/pallas_call | solution.py:345
  68.5 2.3 %copy.5 = f32[1,8,2,128,128]{4,3,2,1,0:T(8,128)} copy(f32[1,8,2,128,128]{4,3,2,1,0:T(8,128)} %self_energy.1) | data formatting | bytes 2097152

commit v3 on v2

--- a/solution.py
+++ b/solution.py
@@ -10,6 +10,9 @@
 NE = 8
 NW = 8
 GROUP = 2
+RUN = 8
+WHOLE = NE - 2
+RELAYED = 4
 MESH = pl.DeviceIdType.MESH
 FAR_UP, FAR_DOWN, NEAR_UP, NEAR_DOWN = range(4)
 HOPS = (2, -2, 1, -1)
@@ -21,7 +24,7 @@
     sizes, green_hbm, screened_hbm, table_hbm, out_hbm,
     table, green, screened, tables, src, rcv, give, take, total, mirror, result, work,
     load_sem, table_send, table_recv, ring_send, ring_recv, pair_send, pair_recv,
-    mirror_send, mirror_recv, out_sem,
+    mirror_send, mirror_recv, relay_send, relay_recv, out_sem,
 ):
     n_ka = sizes["ka"]
     k, r, c = lax.axis_index("ka"), lax.axis_index("br"), lax.axis_index("bc")
@@ -29,17 +32,44 @@
     is_near = (r // GROUP == c // GROUP) & (r != c)
     is_far = r // GROUP != c // GROUP
     partner = (k, c, r)
+    at_run_start = lax.rem(k, RUN) == 0
+    at_run_end = lax.rem(k, RUN) == RUN - 1
+    at_edge = at_run_start | at_run_end
+    far_first = (1 - c // GROUP) * GROUP
 
     def at_hop(hop):
         return (lax.rem(k + hop + n_ka, n_ka), r, c)
 
     barrier = pltpu.get_barrier_semaphore()
+
+    def greet(device):
+        pl.semaphore_signal(barrier, inc=1, device_id=device, device_id_type=MESH)
+
     for hop in HOPS:
-        pl.semaphore_signal(barrier, inc=1, device_id=at_hop(hop), device_id_type=MESH)
+        greet(at_hop(hop))
 
     @pl.when(jnp.logical_not(is_diag))
     def _():
-        pl.semaphore_signal(barrier, inc=1, device_id=partner, device_id_type=MESH)
+        greet(partner)
+
+    @pl.when(is_far & at_edge)
+    def _():
+        greet((k, c, c))
+        greet((k, r, r))
+
+    @pl.when(is_far & at_run_start)
+    def _():
+        greet((at_hop(-1)[0], c, r))
+
+    @pl.when(is_far & at_run_end)
+    def _():
+        greet((at_hop(1)[0], c, r))
+
+    @pl.when(is_diag & at_edge)
+    def _():
+        for q in range(GROUP):
+            greet((k, far_first + q, c))
+            greet((k, c, far_first + q))
 
     loads = [
         pltpu.make_async_copy(green_hbm.at[0], green, load_sem.at[0]),
@@ -49,13 +79,21 @@
     for load in loads:
         load.start()
 
-    @pl.when(is_diag)
+    @pl.when(is_diag & jnp.logical_not(at_edge))
     def _():
         pl.semaphore_wait(barrier, len(HOPS))
 
-    @pl.when(jnp.logical_not(is_diag))
+    @pl.when(is_diag & at_edge)
+    def _():
+        pl.semaphore_wait(barrier, len(HOPS) + 2 * GROUP)
+
+    @pl.when(is_near | (is_far & jnp.logical_not(at_edge)))
     def _():
         pl.semaphore_wait(barrier, len(HOPS) + 1)
+
+    @pl.when(is_far & at_edge)
+    def _():
+        pl.semaphore_wait(barrier, len(HOPS) + 4)
 
     def table_copy(i):
         return pltpu.make_async_remote_copy(
@@ -135,21 +173,46 @@
         result[e, 1] = (total[e, 1] + other[e, 1].T) * 0.5
         out_copy(e).start()
 
+    piece = tile_rows // 2
+
+    def at(u):
+        return lax.div(u, 2), pl.multiple_of(lax.rem(u, 2) * piece, piece)
+
     @pl.when(is_far)
     def _():
-        piece = tile_rows // 2
-        pieces = 2 * NE
-
-        def at(u):
-            return lax.div(u, 2), pl.multiple_of(lax.rem(u, 2) * piece, piece)
+        slots_used = WHOLE + 1
+        pieces = 2 * slots_used
+        mine = jnp.where(r < c, WHOLE, WHOLE + 1)
+        theirs = 2 * WHOLE + 1 - mine
+
+        def crosses(d, j, sending):
+            rising = STEPS[d] > 0
+            edge = at_run_end if rising == sending else at_run_start
+            return edge & (lax.rem(j, 2) == 1)
 
         def ring_piece(d, u):
-            e, start = at(u)
+            j, start = at(u)
+            turn = crosses(d, j, True).astype(jnp.int32)
             return pltpu.make_async_remote_copy(
-                src_ref=src.at[d, e, :, pl.ds(start, piece)], dst_ref=rcv.at[d, e, :, pl.ds(start, piece)],
+                src_ref=src.at[d, j, :, pl.ds(start, piece)], dst_ref=rcv.at[d, j, :, pl.ds(start, piece)],
                 send_sem=ring_send.at[d, u], recv_sem=ring_recv.at[d, u],
-                device_id=at_hop(STEPS[d]), device_id_type=MESH,
+                device_id=(at_hop(STEPS[d])[0], r + turn * (c - r), c + turn * (r - c)), device_id_type=MESH,
             )
+
+        def arrive(d, u):
+            j, _ = at(u)
+            turned = crosses(d, j, False)
+
+            @pl.when(jnp.logical_not(turned))
+            def _():
+                ring_piece(d, u).wait_recv()
+
+            @pl.when(turned & (lax.rem(u, 2) == 0))
+            def _():
+                for n in range(2):
+                    ring_piece(d, u + n).wait_recv()
+                rcv[d, j, 0] = -rcv[d, j, 0].T
+                rcv[d, j, 1] = rcv[d, j, 1].T
 
         def mirror_piece(u):
             e, start = at(u)
@@ -159,48 +222,110 @@
                 device_id=partner, device_id_type=MESH,
             )
 
+        def relayed_piece(u):
+            e, start = at(u)
+            q = lax.rem(r, GROUP)
+            return pltpu.make_async_remote_copy(
+                src_ref=total.at[e, :, pl.ds(start, piece)],
+                dst_ref=take.at[2 * q + lax.div(e, 4), lax.rem(e, 4), :, pl.ds(start, piece)],
+                send_sem=mirror_send.at[u], recv_sem=relay_recv.at[q, u],
+                device_id=(k, c, c), device_id_type=MESH,
+            )
+
+        def send_mirror(u):
+            relayed = at_edge & (u < 2 * RELAYED)
+
+            @pl.when(relayed)
+            def _():
+                relayed_piece(u).start()
+
+            @pl.when(jnp.logical_not(relayed))
+            def _():
+                mirror_piece(u).start()
+
+        def offer(d):
+            terms([give.at[d, 0]], slots[d], theirs)
+            pair_copy(d, 0).start()
+
+        def joined(d, added):
+            terms([work.at[0]], slots[d], mine, added)
+            pair_copy(d, 0).wait_recv()
+            src[d, WHOLE, 0] = work[0, 0] - take[d, 0, 0].T
+            src[d, WHOLE, 1] = work[0, 1] + take[d, 0, 1].T
+            for n in range(2):
+                ring_piece(d, 2 * WHOLE + n).start()
+
         def step(i):
-            @pl.when(i < pieces)
-            def _():
-                e, start = at(i)
+            @pl.when(i < 2 * WHOLE)
+            def _():
+                j, start = at(i)
                 for d in (FAR_UP, FAR_DOWN):
-                    terms([src.at[d, e]], slots[d], e, None, start, piece)
+                    terms([src.at[d, j]], slots[d], j, None, start, piece)
                     ring_piece(d, i).start()
 
-            @pl.when((i >= 3) & (i < pieces + 3))
-            def _():
-                u = i - 3
-                e, start = at(u)
+            for d in range(4):
+                @pl.when(i == d + 1)
+                def _():
+                    offer(d)
+
+            @pl.when(i == 2 * WHOLE)
+            def _():
+                for d in (FAR_UP, FAR_DOWN):
+                    joined(d, None)
+
+            @pl.when((i >= 5) & (i < 2 * WHOLE + 5))
+            def _():
+                u = i - 5
+                j, start = at(u)
                 for d in (NEAR_UP, NEAR_DOWN):
-                    ring_piece(d - 2, u).wait_recv()
-                    terms([src.at[d, e]], slots[d], e, rcv.at[d - 2, e], start, piece)
+                    arrive(d - 2, u)
+                    terms([src.at[d, j]], slots[d], j, rcv.at[d - 2, j], start, piece)
                     ring_piece(d, u).start()
 
-            @pl.when((i >= 6) & (i < pieces + 6))
-            def _():
-                u = i - 6
-                e, start = at(u)
+            @pl.when(i == 2 * WHOLE + 5)
+            def _():
+                for d in (NEAR_UP, NEAR_DOWN):
+                    for n in range(2):
+                        ring_piece(d - 2, 2 * WHOLE + n).wait_recv()
+                    joined(d, rcv.at[d - 2, WHOLE])
+
+            @pl.when(i == 6)
+            def _():
+                for n in range(2):
+                    mirror_piece(2 * theirs + n).start()
+
+            @pl.when((i >= 10) & (i < pieces + 10))
+            def _():
+                u = i - 10
+                j, start = at(u)
+                e = jnp.where(j == WHOLE, mine, j)
                 rows = pl.ds(start, piece)
                 for d in (NEAR_UP, NEAR_DOWN):
-                    ring_piece(d, u).wait_recv()
-                total[e, :, rows] = total[e, :, rows] + (rcv[NEAR_UP, e, :, rows] + rcv[NEAR_DOWN, e, :, rows])
-                mirror_piece(u).start()
-
-            @pl.when((i >= 10) & (lax.rem(i, 2) == 0))
-            def _():
-                e = lax.div(i - 10, 2)
+                    arrive(d, u)
+                total[e, :, rows] = total[e, :, rows] + (rcv[NEAR_UP, j, :, rows] + rcv[NEAR_DOWN, j, :, rows])
+                send_mirror(2 * e + lax.rem(u, 2))
+
+            @pl.when((i >= 20) & (i < 20 + 2 * WHOLE) & (lax.rem(i - 20, 2) == 0))
+            def _():
+                e = lax.div(i - 20, 2)
                 for n in range(2):
                     mirror_piece(2 * e + n).wait_recv()
                 write_out(e, mirror)
 
-        each(pieces + 9, step)
+        each(max(20 + 2 * WHOLE - 1, pieces + 10), step)
+        for e in (mine, theirs):
+            for n in range(2):
+                mirror_piece(2 * e + n).wait_recv()
+            write_out(e, mirror)
 
         def close(u):
             for d in range(4):
                 ring_piece(d, u).wait_send()
-            mirror_piece(u).wait_send()
 
         each(pieces, close)
+        each(2 * NE, lambda u: mirror_piece(u).wait_send())
+        for d in range(4):
+            pair_copy(d, 0).wait_send()
 
     half = NE // 2
 
@@ -305,22 +430,57 @@
                     ring_copy(d - 2, i - 1).wait_recv()
                     folded(d, i - 1, rcv.at[d - 2, i - 1])
 
-            @pl.when(i >= 2)
-            def _():
-                j = i - 2
-                for d in (NEAR_UP, NEAR_DOWN):
-                    ring_copy(d, j).wait_recv()
-                real = rcv[NEAR_UP, j, 0] + rcv[NEAR_DOWN, j, 0]
-                imag = rcv[NEAR_UP, j, 1] + rcv[NEAR_DOWN, j, 1]
-                zero = jnp.zeros_like(real)
-                total[2 * j, 0] = total[2 * j, 0] + jnp.where(row < col, real, zero)
-                total[2 * j, 1] = total[2 * j, 1] + jnp.where(row < col, imag, jnp.where(row == col, imag * 0.5, zero))
-                total[2 * j + 1, 0] = total[2 * j + 1, 0] + jnp.where(row > col, real, zero)
-                total[2 * j + 1, 1] = total[2 * j + 1, 1] + jnp.where(row > col, imag, jnp.where(row == col, real * 0.5, zero))
-                for n in range(2):
-                    write_out(2 * j + n, total)
-
-        each(half + 2, step)
+        def finish(j):
+            for d in (NEAR_UP, NEAR_DOWN):
+                ring_copy(d, j).wait_recv()
+            real = rcv[NEAR_UP, j, 0] + rcv[NEAR_DOWN, j, 0]
+            imag = rcv[NEAR_UP, j, 1] + rcv[NEAR_DOWN, j, 1]
+            zero = jnp.zeros_like(real)
+            total[2 * j, 0] = total[2 * j, 0] + jnp.where(row < col, real, zero)
+            total[2 * j, 1] = total[2 * j, 1] + jnp.where(row < col, imag, jnp.where(row == col, imag * 0.5, zero))
+            total[2 * j + 1, 0] = total[2 * j + 1, 0] + jnp.where(row > col, real, zero)
+            total[2 * j + 1, 1] = total[2 * j + 1, 1] + jnp.where(row > col, imag, jnp.where(row == col, real * 0.5, zero))
+            for n in range(2):
+                write_out(2 * j + n, total)
+
+        each(half + 1, step)
+
+        def passed_on(q, u):
+            e, start = at(u)
+            return pltpu.make_async_remote_copy(
+                src_ref=take.at[2 * q + lax.div(e, 4), lax.rem(e, 4), :, pl.ds(start, piece)],
+                dst_ref=mirror.at[e, :, pl.ds(start, piece)],
+                send_sem=relay_send.at[q, u], recv_sem=mirror_recv.at[u],
+                device_id=(k, c, far_first + q), device_id_type=MESH,
+            )
+
+        def came_in(q, u):
+            e, start = at(u)
+            held = take.at[2 * q + lax.div(e, 4), lax.rem(e, 4), :, pl.ds(start, piece)]
+            return pltpu.make_async_remote_copy(
+                src_ref=total.at[e, :, pl.ds(start, piece)], dst_ref=held,
+                send_sem=relay_send.at[q, u], recv_sem=relay_recv.at[q, u],
+                device_id=(k, far_first + q, c), device_id_type=MESH,
+            )
+
+        @pl.when(at_edge)
+        def _():
+            def relay(u):
+                for q in range(GROUP):
+                    came_in(q, u).wait_recv()
+                    passed_on(q, u).start()
+
+            each(2 * RELAYED, relay)
+
+        each(half, finish)
+
+        @pl.when(at_edge)
+        def _():
+            def relayed(u):
+                for q in range(GROUP):
+                    passed_on(q, u).wait_send()
+
+            each(2 * RELAYED, relayed)
 
         def close(j):
             for d in range(4):
@@ -369,6 +529,8 @@
                 dma((4, half)),
                 dma((2 * NE,)),
                 dma((2 * NE,)),
+                dma((2, 2 * NE)),
+                dma((2, 2 * NE)),
                 dma((NE,)),
             ],
             compiler_params=pltpu.CompilerParams(

time: 70.9 us -> 68.2 us (0.962)
  Pallas kernels: 68.5 us -> 65.2 us
    pallas_call x1, Pallas kernels: 68.5 us -> 65.2 us  [on_device(): pl.pallas_call(functools.partial(kernel, sizes), out_shape=jax.ShapeDtype...]
where the time goes in v3:
time: 68.2 us; the launch traced here: 67.5 us
  Pallas kernels  65.2 us (96%)
  local copies, waits for them, and re-layouts  2.3 us (3%)
    pallas_call x1, Pallas kernels, on_device(): pl.pallas_call(functools.partial(kernel, sizes), out_shape=jax.ShapeDtype...  65.2 us
    unnamed x1, local copies, waits for them, and re-layouts  2.3 us

profile of v3, /device:TPU:5, one launch (start us, length us, event | category | flops | bytes accessed | tf_op | source)
XLA Modules:
  0.0 67.5 jit_solution(9128455064305722194)
XLA Ops:
  0.0 65.2 %self_energy.1 = f32[1,8,2,128,128]{4,3,2,1,0:T(8,128)} custom-call(f32[1,15,2,128,128]{4,3,2,1,0:T(8,128)} %green_hbm.1, f32[5,8,2,128,128]{4,3,2,1,0:T(8,128)} %screened_hbm.1, s32[1,1,5]{2,1,0:T(1,128)} %bitcast.1), custom_call_target="tpu_custom_call" | custom-call | tf_op jit(solution)/shard_map/self_energy/pallas_call | solution.py:505
  65.2 2.3 %copy.5 = f32[1,8,2,128,128]{4,3,2,1,0:T(8,128)} copy(f32[1,8,2,128,128]{4,3,2,1,0:T(8,128)} %self_energy.1) | data formatting | bytes 2097152
